TPU v7x, 512 devices: a whole 4x8x8 slice. The times are simulated.
512 devices in a mesh: ctx: 16 (over y, core), head: 8 (over z), rep: 4 (over x).
Axes of the slice: x: 4, y: 8, z: 8, core: 2. Of those that a mesh axis runs over, the one named last changes fastest.
Arguments:
- q_turn: bfloat16 [1024, 8192], P(('rep', 'ctx', 'head')), parts along dimension 0, may hold values from -18 to 18
- k_turn: bfloat16 [1024, 1024], P(('rep', 'ctx', 'head')), parts along dimension 0, may hold values from -6 to 6
- v_turn: bfloat16 [1024, 1024], P(('rep', 'ctx', 'head')), parts along dimension 0, may hold values from -6 to 6
- cache_k: bfloat16 [2048, 64, 1024], P(('rep', 'ctx'), None, 'head'), parts along dimension 0, may hold values from -6 to 6
- cache_v: bfloat16 [2048, 64, 1024], P(('rep', 'ctx'), None, 'head'), parts along dimension 0, may hold values from -6 to 6
- k_scale: float32 [2048, 8], P(('rep', 'ctx'), 'head'), parts along dimension 0, may hold values from 0.25 to 2
- v_scale: float32 [2048, 8], P(('rep', 'ctx'), 'head'), parts along dimension 0, may hold values from 0.25 to 2
- page_map: int32 [2048], P(('rep', 'ctx')), parts along dimension 0, may hold values from 0 to 511, as said below
Outputs:
- attn_out: bfloat16 [1024, 8192], P(('rep', 'ctx'), 'head'), parts along dimension 0
- cache_k_paired: bfloat16 [131072, 1024], P(('rep', 'ctx'), 'head'), parts along dimension 0
- cache_v_paired: bfloat16 [131072, 1024], P(('rep', 'ctx'), 'head'), parts along dimension 0
There are 4 independent parts, one for each index of `rep`. A program takes and returns all parts, laid end to end along the dimension named above; each array names one. Nothing has to cross between parts.
Inputs may be any that keep to these rules, and one draw needn't show every extreme that they name: A permutation: slot s holds logical page page_map[s]. Cut the 512 logical pages into 32 blocks of 16 consecutive pages; the 32 slots of each index of ctx hold exactly one page of every block.
All inputs are finite; a program needn't handle non-finite values.
Results may differ from a plain program's by a relative error of at most 0.0087.
Values may be sent and summed in bfloat16 or wider, within the bound.
No kernel may reach another device: no remote copies, remote signals or barrier semaphores. Data moves between devices by JAX's collectives and lax.ppermute only.
A program may use at most 64 MiB of HBM per device.

v0:
```python
import math
import jax
import jax.numpy as jnp
from jax import lax
from jax.sharding import PartitionSpec as P


def sent_to_all(shard, axis):
    copies = jnp.broadcast_to(shard, (lax.axis_size(axis), *shard.shape))
    return lax.all_to_all(copies, axis, split_axis=0, concat_axis=0, tiled=True)


def joined_along(tiles, dim):
    lengths = list(tiles.shape[1:])
    lengths[dim] *= tiles.shape[0]
    return jnp.moveaxis(tiles, 0, dim).reshape(lengths)


def collect(shard, axis, dim):
    tiles = sent_to_all(shard, axis)
    return joined_along(tiles, dim)


def sent_together(arrays, axis, split_dim, concat_dim, along):
    both = jnp.concatenate(arrays, axis=along)
    whole, at, done = (
        lax.all_to_all(both, axis, split_axis=split_dim, concat_axis=concat_dim, tiled=True),
        0,
        [],
    )
    for a in arrays:
        done.append(lax.slice_in_dim(whole, at, at + a.shape[along], axis=along))
        at += a.shape[along]
    return tuple(done)


def scale_pages(codes, scales):
    slots, page_rows, width = codes.shape
    heads = scales.shape[1]
    full = (
        codes.astype(jnp.float32).reshape(slots, page_rows, heads, width // heads)
        * scales[:, None, :, None]
    )
    return full.reshape(slots, page_rows, width).astype(jnp.bfloat16)


def attend(queries, keys, values, turn_keys, turn_values, key_start, head_dim):
    length = queries.shape[0]
    q_heads = queries.shape[1] // head_dim
    kv_heads = keys.shape[1] // head_dim
    per_group = q_heads // kv_heads
    factor = 1.0 / math.sqrt(head_dim)
    by_head = queries.reshape(length, q_heads, head_dim).transpose(1, 0, 2)
    cache_kh = keys.reshape(keys.shape[0], kv_heads, head_dim)
    cache_vh = values.reshape(values.shape[0], kv_heads, head_dim)
    turn_kh = turn_keys.reshape(turn_keys.shape[0], kv_heads, head_dim)
    turn_vh = turn_values.reshape(turn_values.shape[0], kv_heads, head_dim)
    places = key_start + jnp.arange(turn_keys.shape[0], dtype=jnp.int32)
    visible = places[None, :] <= jnp.arange(length, dtype=jnp.int32)[:, None]
    dims = (((1,), (1,)), ((), ()))

    def one_head(pair):
        query, index = pair
        kv_index = index // per_group
        ck = lax.dynamic_index_in_dim(cache_kh, kv_index, 1, keepdims=False)
        cv = lax.dynamic_index_in_dim(cache_vh, kv_index, 1, keepdims=False)
        tk = lax.dynamic_index_in_dim(turn_kh, kv_index, 1, keepdims=False)
        tv = lax.dynamic_index_in_dim(turn_vh, kv_index, 1, keepdims=False)
        cached = lax.dot_general(query, ck, dims, preferred_element_type=jnp.float32) * factor
        recent = lax.dot_general(query, tk, dims, preferred_element_type=jnp.float32) * factor
        recent = jnp.where(visible, recent, -jnp.inf)
        peak = jnp.maximum(jnp.max(cached, axis=1), jnp.max(recent, axis=1))
        cached_e = jnp.exp(cached - peak[:, None])
        recent_e = jnp.exp(recent - peak[:, None])
        total = jnp.sum(cached_e, axis=1) + jnp.sum(recent_e, axis=1)
        mixed = jnp.dot(cached_e.astype(jnp.bfloat16), cv, preferred_element_type=jnp.float32)
        mixed = mixed + jnp.dot(
            recent_e.astype(jnp.bfloat16), tv, preferred_element_type=jnp.float32
        )
        return (mixed, peak, total)

    mixed, peak, total = lax.map(one_head, (by_head, jnp.arange(q_heads, dtype=jnp.int32)))
    return (mixed.transpose(1, 0, 2), peak.T, total.T)


def local(q_turn, k_turn, v_turn, cache_k, cache_v, k_scale, v_scale, page_map):
    ctx_count = lax.axis_size("ctx")
    position = lax.axis_index("ctx")
    slots, page_rows, width = cache_k.shape
    head_dim = width // k_scale.shape[1]
    half = slots // 2
    total_pages = slots * ctx_count
    per_peer = slots // ctx_count
    q_mine, k_mine, v_mine = (
        lax.all_to_all(q_turn, "head", split_axis=1, concat_axis=0, tiled=True),
        lax.all_to_all(k_turn, "head", split_axis=1, concat_axis=0, tiled=True),
        lax.all_to_all(v_turn, "head", split_axis=1, concat_axis=0, tiled=True),
    )
    queries = lax.all_gather(q_mine, "ctx", axis=0, tiled=True)
    own_rows = k_mine.shape[0]
    key_start = position * own_rows
    scaled_k = scale_pages(cache_k, k_scale)
    scaled_v = scale_pages(cache_v, v_scale)

    def owner_of(pages):
        block = pages // half
        return jnp.where(block < ctx_count, block, 2 * ctx_count - 1 - block)

    order = jnp.argsort(owner_of(page_map) * total_pages + page_map)
    send_k = scaled_k[order].reshape(slots * page_rows, width)
    send_v = scaled_v[order].reshape(slots * page_rows, width)
    every_map = collect(page_map, "ctx", 0)
    recv_k, recv_v = sent_together((send_k, send_v), "ctx", 0, 0, 1)
    maps = every_map.reshape(ctx_count, slots)
    mine = owner_of(maps) == position
    ranked = jnp.sort(jnp.where(mine, maps, maps + total_pages), axis=1)[:, :per_peer]
    arrived = ranked.reshape(slots)
    within = arrived % half
    place = jnp.where(arrived // half == position, within, half + within)
    back = jnp.argsort(place)
    paired_k = recv_k.reshape(slots, page_rows, width)[back].reshape(slots * page_rows, width)
    paired_v = recv_v.reshape(slots, page_rows, width)[back].reshape(slots * page_rows, width)
    mixed, peak, total = attend(
        queries,
        scaled_k.reshape(slots * page_rows, width),
        scaled_v.reshape(slots * page_rows, width),
        k_mine,
        v_mine,
        key_start,
        head_dim,
    )
    mixed_x, peak_x, total_x = (
        lax.all_to_all(mixed[:, None], "ctx", split_axis=0, concat_axis=1, tiled=True),
        lax.all_to_all(peak[:, None], "ctx", split_axis=0, concat_axis=1, tiled=True),
        lax.all_to_all(total[:, None], "ctx", split_axis=0, concat_axis=1, tiled=True),
    )
    peak_top = jnp.max(peak_x, axis=1)
    weights = jnp.exp(peak_x - peak_top[:, None])
    total_own = jnp.sum(total_x * weights, axis=1)
    mixed_own = jnp.sum(mixed_x * weights[..., None], axis=1)
    attn_out = (mixed_own / total_own[..., None]).reshape(own_rows, -1).astype(jnp.bfloat16)
    return (attn_out, paired_k, paired_v)


def solution(mesh):
    return jax.shard_map(
        local,
        mesh=mesh,
        in_specs=(
            P(("rep", "ctx", "head"), None),
            P(("rep", "ctx", "head"), None),
            P(("rep", "ctx", "head"), None),
            P(("rep", "ctx"), None, "head"),
            P(("rep", "ctx"), None, "head"),
            P(("rep", "ctx"), "head"),
            P(("rep", "ctx"), "head"),
            P(("rep", "ctx")),
        ),
        out_specs=(P(("rep", "ctx"), "head"), P(("rep", "ctx"), "head"), P(("rep", "ctx"), "head")),
        check_vma=False,
    )
```

profile of v0, /device:TPU:1, one launch (start us, length us, event | category | flops | bytes accessed | tf_op | source)
XLA Modules:
  0.0 218.2 jit_solution(17984911208036107442)
XLA Ops:
  0.6 10.9 %all-to-all-start = ((bf16[2,8,1024]{2,0,1:T(2,128)(2,1)}), bf16[2,8,1024]{2,0,1:T(2,128)(2,1)S(1)}, u32[]{:S(2)}, u32[]{:S(2)}) async-start(bf16[2,8,1024]{2,0,1:T(2,128)(2,1)} %bitcast.152), calls=%async_computation | async-start | bytes 65536 | tf_op jit(solution)/shard_map/all_to_all | solution.py:95
  11.5 0.7 fusion.31
  12.2 1.2 multiply_convert_fusion
  13.4 1.2 multiply_convert_fusion.1
  14.6 1.6 sort.46
  16.2 2.2 all-to-all-done
  18.4 4.5 %all-to-all-start.2 = ((bf16[2,8,128]{2,0,1:T(2,128)(2,1)}), bf16[2,8,128]{2,0,1:T(2,128)(2,1)S(1)}, u32[]{:S(2)}, u32[]{:S(2)}) async-start(bf16[2,8,128]{2,0,1:T(2,128)(2,1)} %bitcast.11), calls=%async_computation.2 | async-start | bytes 8192 | tf_op jit(solution)/shard_map/all_to_all | solution.py:97
  22.9 6.4 %all-to-all-done.2 = bf16[2,8,128]{2,0,1:T(2,128)(2,1)S(1)} async-done(((bf16[2,8,128]{2,0,1:T(2,128)(2,1)}), bf16[2,8,128]{2,0,1:T(2,128)(2,1)S(1)}, u32[]{:S(2)}, u32[]{:S(2)}) %all-to-all-start.2) | async-done | bytes 4128 | tf_op jit(solution)/shard_map/all_to_all | solution.py:97
  29.4 3.3 %all-to-all-start.1 = ((bf16[2,8,128]{2,0,1:T(2,128)(2,1)}), bf16[2,8,128]{2,0,1:T(2,128)(2,1)S(1)}, u32[]{:S(2)}, u32[]{:S(2)}) async-start(bf16[2,8,128]{2,0,1:T(2,128)(2,1)} %bitcast.6), calls=%async_computation.1 | async-start | bytes 8192 | tf_op jit(solution)/shard_map/all_to_all | solution.py:96
  32.7 21.5 %all_gather.3 = bf16[256,1024]{1,0:T(8,128)(2,1)S(1)} all-gather(bf16[16,1024]{1,0:T(8,128)(2,1)S(1)} %all_to_all.92), channel_id=1, replica_groups=mesh['ctx'=16,'head'=8,'rep'=4] {'ctx'}, dimensions={0}, use_global_device_ids=true | all-gather | bytes 557056 | tf_op jit(solution)/shard_map/all_gather | solution.py:99
  54.2 1.0 copy.33
  55.2 0.6 broadcast_in_dim.50
  55.8 4.5 %all-to-all-start.7 = ((s32[16,1,32]{2,1,0:T(1,128)}), s32[16,1,32]{2,1,0:T(1,128)S(1)}, u32[]{:S(2)}, u32[]{:S(2)}) async-start(s32[16,1,32]{2,1,0:T(1,128)} %broadcast_in_dim.50), calls=%async_computation.7 | async-start | bytes 16384 | tf_op jit(solution)/shard_map/all_to_all | solution.py:10
  60.3 66.8 %while.16 = (s32[]{:T(128)}, f32[8,256,128]{2,0,1:T(8,128)}, f32[8,256]{1,0:T(8,128)S(1)}, f32[8,256]{1,0:T(8,128)S(1)}, bf16[8,256,128]{1,2,0:T(8,128)(2,1)}, /...) while((s32[]{:T(128)}, f32[8,256,128]{2,0,1:T(8,128)}, ...), condition=%wide.region_5.6_spmd.clone, body=%wide.region_0.5_spmd.clone.sunk | while | flops 273743360 | bytes 8203457 | solution.py:82
  60.3 1.0 fusion.50
  61.3 1.4 fusion.51
  63.4 0.5 convolution_add_fusion.2
  64.0 4.7 %dynamic_update_slice.20 = f32[8,256,128]{2,0,1:T(8,128)} dynamic-update-slice(f32[8,256,128]{2,0,1:T(8,128)} %get-tuple-element.254, f32[1,256,128]{2,0,1:T(1,128)S(1)} %bitcast.134, s32[]{:T(128)} %get-tuple-element.253, s32[]{:T(128)} %constant.101.clone.1..sunk, s32[]{:T(128)} %constant.101.clone.1..sunk) | dynamic-update-slice | bytes 262148 | tf_op jit(solution)/shard_map/while/body/jit(dynamic_update_index_in_dim)/dynamic_update_slice | solution.py:82
  68.7 1.0 fusion.50
  69.6 1.4 fusion.51
  71.8 0.5 convolution_add_fusion.2
  72.3 4.7 %dynamic_update_slice.20 = f32[8,256,128]{2,0,1:T(8,128)} dynamic-update-slice(f32[8,256,128]{2,0,1:T(8,128)} %get-tuple-element.254, f32[1,256,128]{2,0,1:T(1,128)S(1)} %bitcast.134, s32[]{:T(128)} %get-tuple-element.253, s32[]{:T(128)} %constant.101.clone.1..sunk, s32[]{:T(128)} %constant.101.clone.1..sunk) | dynamic-update-slice | bytes 262148 | tf_op jit(solution)/shard_map/while/body/jit(dynamic_update_index_in_dim)/dynamic_update_slice | solution.py:82
  77.0 1.0 fusion.50
  78.0 1.4 fusion.51
  80.7 4.7 %dynamic_update_slice.20 = f32[8,256,128]{2,0,1:T(8,128)} dynamic-update-slice(f32[8,256,128]{2,0,1:T(8,128)} %get-tuple-element.254, f32[1,256,128]{2,0,1:T(1,128)S(1)} %bitcast.134, s32[]{:T(128)} %get-tuple-element.253, s32[]{:T(128)} %constant.101.clone.1..sunk, s32[]{:T(128)} %constant.101.clone.1..sunk) | dynamic-update-slice | bytes 262148 | tf_op jit(solution)/shard_map/while/body/jit(dynamic_update_index_in_dim)/dynamic_update_slice | solution.py:82
  85.4 1.0 fusion.50
  86.4 1.4 fusion.51
  88.5 0.5 convolution_add_fusion.2
  89.0 4.7 %dynamic_update_slice.20 = f32[8,256,128]{2,0,1:T(8,128)} dynamic-update-slice(f32[8,256,128]{2,0,1:T(8,128)} %get-tuple-element.254, f32[1,256,128]{2,0,1:T(1,128)S(1)} %bitcast.134, s32[]{:T(128)} %get-tuple-element.253, s32[]{:T(128)} %constant.101.clone.1..sunk, s32[]{:T(128)} %constant.101.clone.1..sunk) | dynamic-update-slice | bytes 262148 | tf_op jit(solution)/shard_map/while/body/jit(dynamic_update_index_in_dim)/dynamic_update_slice | solution.py:82
  93.7 1.0 fusion.50
  94.7 1.4 fusion.51
  96.9 0.5 convolution_add_fusion.2
  97.4 4.7 %dynamic_update_slice.20 = f32[8,256,128]{2,0,1:T(8,128)} dynamic-update-slice(f32[8,256,128]{2,0,1:T(8,128)} %get-tuple-element.254, f32[1,256,128]{2,0,1:T(1,128)S(1)} %bitcast.134, s32[]{:T(128)} %get-tuple-element.253, s32[]{:T(128)} %constant.101.clone.1..sunk, s32[]{:T(128)} %constant.101.clone.1..sunk) | dynamic-update-slice | bytes 262148 | tf_op jit(solution)/shard_map/while/body/jit(dynamic_update_index_in_dim)/dynamic_update_slice | solution.py:82
  102.1 1.0 fusion.50
  103.1 1.4 fusion.51
  105.7 4.7 %dynamic_update_slice.20 = f32[8,256,128]{2,0,1:T(8,128)} dynamic-update-slice(f32[8,256,128]{2,0,1:T(8,128)} %get-tuple-element.254, f32[1,256,128]{2,0,1:T(1,128)S(1)} %bitcast.134, s32[]{:T(128)} %get-tuple-element.253, s32[]{:T(128)} %constant.101.clone.1..sunk, s32[]{:T(128)} %constant.101.clone.1..sunk) | dynamic-update-slice | bytes 262148 | tf_op jit(solution)/shard_map/while/body/jit(dynamic_update_index_in_dim)/dynamic_update_slice | solution.py:82
  110.4 1.0 fusion.50
  111.4 1.4 fusion.51
  113.6 0.5 convolution_add_fusion.2
  114.1 4.7 %dynamic_update_slice.20 = f32[8,256,128]{2,0,1:T(8,128)} dynamic-update-slice(f32[8,256,128]{2,0,1:T(8,128)} %get-tuple-element.254, f32[1,256,128]{2,0,1:T(1,128)S(1)} %bitcast.134, s32[]{:T(128)} %get-tuple-element.253, s32[]{:T(128)} %constant.101.clone.1..sunk, s32[]{:T(128)} %constant.101.clone.1..sunk) | dynamic-update-slice | bytes 262148 | tf_op jit(solution)/shard_map/while/body/jit(dynamic_update_index_in_dim)/dynamic_update_slice | solution.py:82
  118.8 1.0 fusion.50
  119.8 1.4 fusion.51
  121.9 0.5 convolution_add_fusion.2
  122.5 4.7 %dynamic_update_slice.20 = f32[8,256,128]{2,0,1:T(8,128)} dynamic-update-slice(f32[8,256,128]{2,0,1:T(8,128)} %get-tuple-element.254, f32[1,256,128]{2,0,1:T(1,128)S(1)} %bitcast.134, s32[]{:T(128)} %get-tuple-element.253, s32[]{:T(128)} %constant.101.clone.1..sunk, s32[]{:T(128)} %constant.101.clone.1..sunk) | dynamic-update-slice | bytes 262148 | tf_op jit(solution)/shard_map/while/body/jit(dynamic_update_index_in_dim)/dynamic_update_slice | solution.py:82
  127.8 1.0 reduce.3
  128.8 0.7 reshape.187
  129.5 7.2 %all-to-all-start.4 = ((f32[16,1,128]{2,1,0:T(1,128)}), f32[16,1,128]{2,1,0:T(1,128)S(1)}, u32[]{:S(2)}, u32[]{:S(2)}) async-start(f32[16,1,128]{2,1,0:T(1,128)} %reshape.187), calls=%async_computation.4 | async-start | bytes 16384 | tf_op jit(solution)/shard_map/all_to_all | solution.py:134
  136.7 0.6 gather_fusion
  137.4 0.6 gather_fusion.1
  138.2 1.0 reduce.1
  139.2 0.7 reshape.189
  139.9 3.8 %all-to-all-done.4 = f32[16,1,128]{2,1,0:T(1,128)S(1)} async-done(((f32[16,1,128]{2,1,0:T(1,128)}), f32[16,1,128]{2,1,0:T(1,128)S(1)}, u32[]{:S(2)}, u32[]{:S(2)}) %all-to-all-start.4) | async-done | bytes 8224 | tf_op jit(solution)/shard_map/all_to_all | solution.py:134
  143.7 3.9 %all-to-all-start.5 = ((f32[16,1,128]{2,1,0:T(1,128)}), f32[16,1,128]{2,1,0:T(1,128)S(1)}, u32[]{:S(2)}, u32[]{:S(2)}) async-start(f32[16,1,128]{2,1,0:T(1,128)} %reshape.189), calls=%async_computation.5 | async-start | bytes 16384 | tf_op jit(solution)/shard_map/all_to_all | solution.py:135
  147.8 6.9 %all-to-all-done.5 = f32[16,1,128]{2,1,0:T(1,128)S(1)} async-done(((f32[16,1,128]{2,1,0:T(1,128)}), f32[16,1,128]{2,1,0:T(1,128)S(1)}, u32[]{:S(2)}, u32[]{:S(2)}) %all-to-all-start.5) | async-done | bytes 8224 | tf_op jit(solution)/shard_map/all_to_all | solution.py:135
  154.6 31.6 %all_to_all.123 = bf16[16,128,256]{2,1,0:T(8,128)(2,1)S(1)} all-to-all(bf16[16,128,256]{2,1,0:T(8,128)(2,1)S(1)} %pad_maximum_fusion), channel_id=1, replica_groups=mesh['ctx'=16,'head'=8,'rep'=4] {'ctx'}, dimensions={0} | all-to-all | bytes 2097152 | tf_op jit(solution)/shard_map/all_to_all | solution.py:27
  186.3 3.6 %all-to-all-start.3 = ((f32[256,1,8,128]{3,2,1,0:T(8,128)}), f32[256,1,8,128]{3,2,1,0:T(8,128)S(1)}, u32[]{:S(2)}, u32[]{:S(2)}) async-start(f32[256,1,8,128]{3,2,1,0:T(8,128)} %bitcast.15), calls=%async_computation.3 | async-start | bytes 2097152 | tf_op jit(solution)/shard_map/all_to_all | solution.py:133
  189.9 0.8 sort.47
  190.9 1.6 sort.48
  192.6 0.7 reduce.4
  193.6 0.7 reduce.2
  194.8 1.4 gather_fusion.2
  196.2 1.4 gather_fusion.3
  197.6 19.5 %all-to-all-done.3 = f32[256,1,8,128]{3,2,1,0:T(8,128)S(1)} async-done(((f32[256,1,8,128]{3,2,1,0:T(8,128)}), f32[256,1,8,128]{3,2,1,0:T(8,128)S(1)}, u32[]{:S(2)}, u32[]{:S(2)}) %all-to-all-start.3) | async-done | bytes 1048608 | tf_op jit(solution)/shard_map/all_to_all | solution.py:133
  217.5 0.7 copy_bitcast_fusion
  (92 shorter events, 9.4 us)
Async XLA Ops:
  0.6 54.6 %copy-start = (s32[32]{0:T(128)S(1)}, s32[32]{0:T(128)}, u32[]{:S(2)}) copy-start(s32[32]{0:T(128)} %param.17) | copy-start | bytes 388
  0.6 17.7 %all-to-all-start = ((bf16[2,8,1024]{2,0,1:T(2,128)(2,1)}), bf16[2,8,1024]{2,0,1:T(2,128)(2,1)S(1)}, u32[]{:S(2)}, u32[]{:S(2)}) async-start(bf16[2,8,1024]{2,0,1:T(2,128)(2,1)} %bitcast.152), calls=%async_computation | async-start | bytes 65536 | tf_op jit(solution)/shard_map/all_to_all | solution.py:95
  18.4 11.0 %all-to-all-start.2 = ((bf16[2,8,128]{2,0,1:T(2,128)(2,1)}), bf16[2,8,128]{2,0,1:T(2,128)(2,1)S(1)}, u32[]{:S(2)}, u32[]{:S(2)}) async-start(bf16[2,8,128]{2,0,1:T(2,128)(2,1)} %bitcast.11), calls=%async_computation.2 | async-start | bytes 8192 | tf_op jit(solution)/shard_map/all_to_all | solution.py:97
  29.4 25.8 %all-to-all-start.1 = ((bf16[2,8,128]{2,0,1:T(2,128)(2,1)}), bf16[2,8,128]{2,0,1:T(2,128)(2,1)S(1)}, u32[]{:S(2)}, u32[]{:S(2)}) async-start(bf16[2,8,128]{2,0,1:T(2,128)(2,1)} %bitcast.6), calls=%async_computation.1 | async-start | bytes 8192 | tf_op jit(solution)/shard_map/all_to_all | solution.py:96
  55.8 73.7 %all-to-all-start.7 = ((s32[16,1,32]{2,1,0:T(1,128)}), s32[16,1,32]{2,1,0:T(1,128)S(1)}, u32[]{:S(2)}, u32[]{:S(2)}) async-start(s32[16,1,32]{2,1,0:T(1,128)} %broadcast_in_dim.50), calls=%async_computation.7 | async-start | bytes 16384 | tf_op jit(solution)/shard_map/all_to_all | solution.py:10
  129.5 14.2 %all-to-all-start.4 = ((f32[16,1,128]{2,1,0:T(1,128)}), f32[16,1,128]{2,1,0:T(1,128)S(1)}, u32[]{:S(2)}, u32[]{:S(2)}) async-start(f32[16,1,128]{2,1,0:T(1,128)} %reshape.187), calls=%async_computation.4 | async-start | bytes 16384 | tf_op jit(solution)/shard_map/all_to_all | solution.py:134
  143.7 10.9 %all-to-all-start.5 = ((f32[16,1,128]{2,1,0:T(1,128)}), f32[16,1,128]{2,1,0:T(1,128)S(1)}, u32[]{:S(2)}, u32[]{:S(2)}) async-start(f32[16,1,128]{2,1,0:T(1,128)} %reshape.189), calls=%async_computation.5 | async-start | bytes 16384 | tf_op jit(solution)/shard_map/all_to_all | solution.py:135
  186.3 30.9 %all-to-all-start.3 = ((f32[256,1,8,128]{3,2,1,0:T(8,128)}), f32[256,1,8,128]{3,2,1,0:T(8,128)S(1)}, u32[]{:S(2)}, u32[]{:S(2)}) async-start(f32[256,1,8,128]{3,2,1,0:T(8,128)} %bitcast.15), calls=%async_computation.3 | async-start | bytes 2097152 | tf_op jit(solution)/shard_map/all_to_all | solution.py:133
where the time goes:
time: 220 us; the launch traced here: 218 us
  blocking collectives  53.2 us (24%)
  local copies, waits for them, and re-layouts  46.7 us (21%)
  waiting for transfers between devices  38.8 us (18%)
  starting transfers between devices  37.9 us (17%)
  matrix products  24.9 us (11%)
  other arithmetic  15.5 us (7%)
    dynamic_update_slice x24, local copies, waits for them, and re-layouts, attend(): lax.map(one_head, (by_head, jnp.arange(q_heads, dtype=jnp.int32)))  37.8 us
    all_to_all x1, blocking collectives, sent_together(): lax.all_to_all(both, axis, split_axis=split_dim, concat_axis=concat_dim,...  31.6 us
    all_gather x1, blocking collectives, local(): queries = lax.all_gather(q_mine, 'ctx', axis=0, tiled=True)  21.5 us
    all_to_all x1, waiting for transfers between devices, local(): lax.all_to_all(mixed[:, None], 'ctx', split_axis=0, concat_axis=1, tiled=...  19.5 us
    dot_general x8, matrix products, one_head(): lax.dot_general(query, ck, dims, preferred_element_type=jnp.float32)  11.1 us
    all_to_all x1, starting transfers between devices, local(): lax.all_to_all(q_turn, 'head', split_axis=1, concat_axis=0, tiled=True)  10.9 us
    dot_general x8, matrix products, one_head(): lax.dot_general(query, tk, dims, preferred_element_type=jnp.float32)  7.9 us
    all_to_all x1, starting transfers between devices, local(): lax.all_to_all(peak[:, None], 'ctx', split_axis=0, concat_axis=1, tiled=T...  7.23 us
  transfers between devices with their start and end apart: 7, of which 5 were waited for; matrix products, arithmetic and copies ran while one was open for 39% of the time, Pallas kernels for 0%

commit v1 on v0

--- a/solution.py
+++ b/solution.py
@@ -96,7 +96,12 @@
         lax.all_to_all(k_turn, "head", split_axis=1, concat_axis=0, tiled=True),
         lax.all_to_all(v_turn, "head", split_axis=1, concat_axis=0, tiled=True),
     )
-    queries = lax.all_gather(q_mine, "ctx", axis=0, tiled=True)
+    buffer = []
+    for _ in range(lax.axis_size("ctx")):
+        buffer.append(q_mine)
+    queries = jnp.concatenate(
+        lax.all_to_all(jnp.stack(buffer, 0), "ctx", concat_axis=0, split_axis=0), 0
+    )
     own_rows = k_mine.shape[0]
     key_start = position * own_rows
     scaled_k = scale_pages(cache_k, k_scale)

time: 220 us -> 231 us (1.050)
  waiting for transfers between devices: 38.8 us -> 55.9 us
  blocking collectives: 53.2 us -> 49.5 us
    all_gather x1 -> x0, blocking collectives: 21.5 us -> none  [local(): queries = lax.all_gather(q_mine, 'ctx', axis=0, tiled=True)]
    all_to_all x0 -> x1, blocking collectives: none -> 17.9 us  [local(): lax.all_to_all(q_turn, 'head', split_axis=1, concat_axis=0, tiled=True)]
    all_to_all x1, waiting for transfers between devices: 2.15 us -> 13.9 us  [local(): lax.all_to_all(jnp.stack(buffer, 0), 'ctx', concat_axis=0, split_axis=0)]
    all_to_all x1, waiting for transfers between devices: 0.01 us -> 5.37 us  [local(): lax.all_to_all(k_turn, 'head', split_axis=1, concat_axis=0, tiled=True)]
  transfers between devices with their start and end apart: 7 -> 7, of which waited for: 5 -> 6; matrix products, arithmetic and copies ran while one was open for 39% -> 37% of each run, Pallas kernels for 0% -> 0%
where the time goes in v1:
time: 231 us; the launch traced here: 229 us
  waiting for transfers between devices  55.9 us (24%)
  blocking collectives  49.5 us (21%)
  local copies, waits for them, and re-layouts  47.6 us (21%)
  starting transfers between devices  35.8 us (15%)
  matrix products  24.6 us (11%)
  other arithmetic  14.1 us (6%)
    dynamic_update_slice x24, local copies, waits for them, and re-layouts, attend(): lax.map(one_head, (by_head, jnp.arange(q_heads, dtype=jnp.int32)))  37.8 us
    all_to_all x1, blocking collectives, sent_together(): lax.all_to_all(both, axis, split_axis=split_dim, concat_axis=concat_dim,...  31.6 us
    all_to_all x1, waiting for transfers between devices, local(): lax.all_to_all(mixed[:, None], 'ctx', split_axis=0, concat_axis=1, tiled=...  19.5 us
    all_to_all x1, blocking collectives, local(): lax.all_to_all(q_turn, 'head', split_axis=1, concat_axis=0, tiled=True)  17.9 us
    all_to_all x1, waiting for transfers between devices, local(): lax.all_to_all(jnp.stack(buffer, 0), 'ctx', concat_axis=0, split_axis=0)  13.9 us
    dot_general x8, matrix products, one_head(): lax.dot_general(query, ck, dims, preferred_element_type=jnp.float32)  10.9 us
    all_to_all x1, starting transfers between devices, local(): lax.all_to_all(jnp.stack(buffer, 0), 'ctx', concat_axis=0, split_axis=0)  10.4 us
    dot_general x8, matrix products, one_head(): lax.dot_general(query, tk, dims, preferred_element_type=jnp.float32)  8.04 us
  transfers between devices with their start and end apart: 7, of which 6 were waited for; matrix products, arithmetic and copies ran while one was open for 37% of the time, Pallas kernels for 0%

profile of v1, /device:TPU:1, one launch (start us, length us, event | category | flops | bytes accessed | tf_op | source)
XLA Modules:
  0.0 228.7 jit_solution(6597231359951751124)
XLA Ops:
  0.7 17.9 %all_to_all.125 = bf16[2,8,1024]{2,0,1:T(2,128)(2,1)S(1)} all-to-all(bf16[2,8,1024]{2,0,1:T(2,128)(2,1)} %bitcast.154), channel_id=1, replica_groups=mesh['ctx'=16,'head'=8,'rep'=4] {'head'}, dimensions={1} | all-to-all | bytes 65536 | tf_op jit(solution)/shard_map/all_to_all | solution.py:95
  18.5 3.3 %all-to-all-start.3 = ((bf16[2,8,128]{2,0,1:T(2,128)(2,1)}), bf16[2,8,128]{2,0,1:T(2,128)(2,1)S(1)}, u32[]{:S(2)}, u32[]{:S(2)}) async-start(bf16[2,8,128]{2,0,1:T(2,128)(2,1)} %bitcast.155), calls=%async_computation.3 | async-start | bytes 8192 | tf_op jit(solution)/shard_map/all_to_all | solution.py:97
  21.9 6.4 %all-to-all-done.3 = bf16[2,8,128]{2,0,1:T(2,128)(2,1)S(1)} async-done(((bf16[2,8,128]{2,0,1:T(2,128)(2,1)}), bf16[2,8,128]{2,0,1:T(2,128)(2,1)S(1)}, u32[]{:S(2)}, u32[]{:S(2)}) %all-to-all-start.3) | async-done | bytes 4128 | tf_op jit(solution)/shard_map/all_to_all | solution.py:97
  28.2 0.9 stack.5
  29.1 10.4 %all-to-all-start.1 = ((bf16[16,16,1024]{2,1,0:T(8,128)(2,1)}), bf16[16,16,1024]{2,1,0:T(8,128)(2,1)S(1)}, u32[]{:S(2)}, u32[]{:S(2)}) async-start(bf16[16,16,1024]{2,1,0:T(8,128)(2,1)} %stack.5), calls=%async_computation.1 | async-start | bytes 1048576 | tf_op jit(solution)/shard_map/all_to_all | solution.py:103
  39.5 0.7 fusion.31
  40.1 1.6 sort.46
  41.8 0.8 multiply_convert_fusion.1
  42.8 13.9 %all-to-all-done.1 = bf16[16,16,1024]{2,1,0:T(8,128)(2,1)S(1)} async-done(((bf16[16,16,1024]{2,1,0:T(8,128)(2,1)}), bf16[16,16,1024]{2,1,0:T(8,128)(2,1)S(1)}, u32[]{:S(2)}, u32[]{:S(2)}) %all-to-all-start.1) | async-done | bytes 524320 | tf_op jit(solution)/shard_map/all_to_all | solution.py:103
  56.7 3.3 %all-to-all-start.2 = ((bf16[2,8,128]{2,0,1:T(2,128)(2,1)}), bf16[2,8,128]{2,0,1:T(2,128)(2,1)S(1)}, u32[]{:S(2)}, u32[]{:S(2)}) async-start(bf16[2,8,128]{2,0,1:T(2,128)(2,1)} %bitcast.5), calls=%async_computation.2 | async-start | bytes 8192 | tf_op jit(solution)/shard_map/all_to_all | solution.py:96
  60.1 0.9 copy.33
  61.0 5.4 %all-to-all-done.2 = bf16[2,8,128]{2,0,1:T(2,128)(2,1)S(1)} async-done(((bf16[2,8,128]{2,0,1:T(2,128)(2,1)}), bf16[2,8,128]{2,0,1:T(2,128)(2,1)S(1)}, u32[]{:S(2)}, u32[]{:S(2)}) %all-to-all-start.2) | async-done | bytes 4128 | tf_op jit(solution)/shard_map/all_to_all | solution.py:96
  66.4 0.6 broadcast_in_dim.50
  67.0 4.1 %all-to-all-start.8 = ((s32[16,1,32]{2,1,0:T(1,128)}), s32[16,1,32]{2,1,0:T(1,128)S(1)}, u32[]{:S(2)}, u32[]{:S(2)}) async-start(s32[16,1,32]{2,1,0:T(1,128)} %broadcast_in_dim.50), calls=%async_computation.8 | async-start | bytes 16384 | tf_op jit(solution)/shard_map/all_to_all | solution.py:10
  71.1 66.5 %while.16 = (s32[]{:T(128)}, f32[8,256,128]{2,0,1:T(8,128)}, f32[8,256]{1,0:T(8,128)S(1)}, f32[8,256]{1,0:T(8,128)S(1)}, bf16[8,256,128]{2,1,0:T(8,128)(2,1)}, /...) while((s32[]{:T(128)}, f32[8,256,128]{2,0,1:T(8,128)}, ...), condition=%wide.region_5.6_spmd.clone, body=%wide.region_0.5_spmd.clone.sunk | while | flops 273743360 | bytes 8203457 | solution.py:82
  71.1 1.0 fusion.50
  72.1 1.4 fusion.51
  74.2 0.5 convolution_add_fusion.2
  74.8 4.7 %dynamic_update_slice.20 = f32[8,256,128]{2,0,1:T(8,128)} dynamic-update-slice(f32[8,256,128]{2,0,1:T(8,128)} %get-tuple-element.254, f32[1,256,128]{2,0,1:T(1,128)S(1)} %bitcast.134, s32[]{:T(128)} %get-tuple-element.253, s32[]{:T(128)} %constant.101.clone.1..sunk, s32[]{:T(128)} %constant.101.clone.1..sunk) | dynamic-update-slice | bytes 262148 | tf_op jit(solution)/shard_map/while/body/jit(dynamic_update_index_in_dim)/dynamic_update_slice | solution.py:82
  79.5 1.0 fusion.50
  80.5 1.4 fusion.51
  82.6 0.5 convolution_add_fusion.2
  83.1 4.7 %dynamic_update_slice.20 = f32[8,256,128]{2,0,1:T(8,128)} dynamic-update-slice(f32[8,256,128]{2,0,1:T(8,128)} %get-tuple-element.254, f32[1,256,128]{2,0,1:T(1,128)S(1)} %bitcast.134, s32[]{:T(128)} %get-tuple-element.253, s32[]{:T(128)} %constant.101.clone.1..sunk, s32[]{:T(128)} %constant.101.clone.1..sunk) | dynamic-update-slice | bytes 262148 | tf_op jit(solution)/shard_map/while/body/jit(dynamic_update_index_in_dim)/dynamic_update_slice | solution.py:82
  87.8 1.0 fusion.50
  88.8 1.4 fusion.51
  91.4 4.7 %dynamic_update_slice.20 = f32[8,256,128]{2,0,1:T(8,128)} dynamic-update-slice(f32[8,256,128]{2,0,1:T(8,128)} %get-tuple-element.254, f32[1,256,128]{2,0,1:T(1,128)S(1)} %bitcast.134, s32[]{:T(128)} %get-tuple-element.253, s32[]{:T(128)} %constant.101.clone.1..sunk, s32[]{:T(128)} %constant.101.clone.1..sunk) | dynamic-update-slice | bytes 262148 | tf_op jit(solution)/shard_map/while/body/jit(dynamic_update_index_in_dim)/dynamic_update_slice | solution.py:82
  96.1 1.0 fusion.50
  97.1 1.4 fusion.51
  99.7 4.7 %dynamic_update_slice.20 = f32[8,256,128]{2,0,1:T(8,128)} dynamic-update-slice(f32[8,256,128]{2,0,1:T(8,128)} %get-tuple-element.254, f32[1,256,128]{2,0,1:T(1,128)S(1)} %bitcast.134, s32[]{:T(128)} %get-tuple-element.253, s32[]{:T(128)} %constant.101.clone.1..sunk, s32[]{:T(128)} %constant.101.clone.1..sunk) | dynamic-update-slice | bytes 262148 | tf_op jit(solution)/shard_map/while/body/jit(dynamic_update_index_in_dim)/dynamic_update_slice | solution.py:82
  104.4 1.0 fusion.50
  105.4 1.4 fusion.51
  107.5 0.5 convolution_add_fusion.2
  108.0 4.7 %dynamic_update_slice.20 = f32[8,256,128]{2,0,1:T(8,128)} dynamic-update-slice(f32[8,256,128]{2,0,1:T(8,128)} %get-tuple-element.254, f32[1,256,128]{2,0,1:T(1,128)S(1)} %bitcast.134, s32[]{:T(128)} %get-tuple-element.253, s32[]{:T(128)} %constant.101.clone.1..sunk, s32[]{:T(128)} %constant.101.clone.1..sunk) | dynamic-update-slice | bytes 262148 | tf_op jit(solution)/shard_map/while/body/jit(dynamic_update_index_in_dim)/dynamic_update_slice | solution.py:82
  112.7 1.0 fusion.50
  113.7 1.4 fusion.51
  116.3 4.7 %dynamic_update_slice.20 = f32[8,256,128]{2,0,1:T(8,128)} dynamic-update-slice(f32[8,256,128]{2,0,1:T(8,128)} %get-tuple-element.254, f32[1,256,128]{2,0,1:T(1,128)S(1)} %bitcast.134, s32[]{:T(128)} %get-tuple-element.253, s32[]{:T(128)} %constant.101.clone.1..sunk, s32[]{:T(128)} %constant.101.clone.1..sunk) | dynamic-update-slice | bytes 262148 | tf_op jit(solution)/shard_map/while/body/jit(dynamic_update_index_in_dim)/dynamic_update_slice | solution.py:82
  121.0 1.0 fusion.50
  122.0 1.4 fusion.51
  124.6 4.7 %dynamic_update_slice.20 = f32[8,256,128]{2,0,1:T(8,128)} dynamic-update-slice(f32[8,256,128]{2,0,1:T(8,128)} %get-tuple-element.254, f32[1,256,128]{2,0,1:T(1,128)S(1)} %bitcast.134, s32[]{:T(128)} %get-tuple-element.253, s32[]{:T(128)} %constant.101.clone.1..sunk, s32[]{:T(128)} %constant.101.clone.1..sunk) | dynamic-update-slice | bytes 262148 | tf_op jit(solution)/shard_map/while/body/jit(dynamic_update_index_in_dim)/dynamic_update_slice | solution.py:82
  129.3 1.0 fusion.50
  130.3 1.4 fusion.51
  132.4 0.5 convolution_add_fusion.2
  133.0 4.7 %dynamic_update_slice.20 = f32[8,256,128]{2,0,1:T(8,128)} dynamic-update-slice(f32[8,256,128]{2,0,1:T(8,128)} %get-tuple-element.254, f32[1,256,128]{2,0,1:T(1,128)S(1)} %bitcast.134, s32[]{:T(128)} %get-tuple-element.253, s32[]{:T(128)} %constant.101.clone.1..sunk, s32[]{:T(128)} %constant.101.clone.1..sunk) | dynamic-update-slice | bytes 262148 | tf_op jit(solution)/shard_map/while/body/jit(dynamic_update_index_in_dim)/dynamic_update_slice | solution.py:82
  137.8 0.5 broadcast.86
  138.3 1.0 reduce.3
  139.3 0.7 reshape.186
  140.0 7.2 %all-to-all-start.5 = ((f32[16,1,128]{2,1,0:T(1,128)}), f32[16,1,128]{2,1,0:T(1,128)S(1)}, u32[]{:S(2)}, u32[]{:S(2)}) async-start(f32[16,1,128]{2,1,0:T(1,128)} %reshape.186), calls=%async_computation.5 | async-start | bytes 16384 | tf_op jit(solution)/shard_map/all_to_all | solution.py:139
  147.2 0.6 gather_fusion
  147.9 0.6 gather_fusion.1
  148.7 1.0 reduce.1
  149.6 0.7 reshape.188
  150.4 3.8 %all-to-all-done.5 = f32[16,1,128]{2,1,0:T(1,128)S(1)} async-done(((f32[16,1,128]{2,1,0:T(1,128)}), f32[16,1,128]{2,1,0:T(1,128)S(1)}, u32[]{:S(2)}, u32[]{:S(2)}) %all-to-all-start.5) | async-done | bytes 8224 | tf_op jit(solution)/shard_map/all_to_all | solution.py:139
  154.2 3.9 %all-to-all-start.6 = ((f32[16,1,128]{2,1,0:T(1,128)}), f32[16,1,128]{2,1,0:T(1,128)S(1)}, u32[]{:S(2)}, u32[]{:S(2)}) async-start(f32[16,1,128]{2,1,0:T(1,128)} %reshape.188), calls=%async_computation.6 | async-start | bytes 16384 | tf_op jit(solution)/shard_map/all_to_all | solution.py:140
  158.2 6.9 %all-to-all-done.6 = f32[16,1,128]{2,1,0:T(1,128)S(1)} async-done(((f32[16,1,128]{2,1,0:T(1,128)}), f32[16,1,128]{2,1,0:T(1,128)S(1)}, u32[]{:S(2)}, u32[]{:S(2)}) %all-to-all-start.6) | async-done | bytes 8224 | tf_op jit(solution)/shard_map/all_to_all | solution.py:140
  165.1 31.6 %all_to_all.126 = bf16[16,128,256]{2,1,0:T(8,128)(2,1)S(1)} all-to-all(bf16[16,128,256]{2,1,0:T(8,128)(2,1)S(1)} %pad_maximum_fusion), channel_id=1, replica_groups=mesh['ctx'=16,'head'=8,'rep'=4] {'ctx'}, dimensions={0} | all-to-all | bytes 2097152 | tf_op jit(solution)/shard_map/all_to_all | solution.py:27
  196.8 3.6 %all-to-all-start.4 = ((f32[256,1,8,128]{3,2,1,0:T(8,128)}), f32[256,1,8,128]{3,2,1,0:T(8,128)S(1)}, u32[]{:S(2)}, u32[]{:S(2)}) async-start(f32[256,1,8,128]{3,2,1,0:T(8,128)} %bitcast.14), calls=%async_computation.4 | async-start | bytes 2097152 | tf_op jit(solution)/shard_map/all_to_all | solution.py:138
  200.4 0.8 sort.47
  201.4 1.6 sort.48
  203.1 0.7 reduce.4
  204.1 0.7 reduce.2
  205.3 1.4 gather_fusion.2
  206.7 1.4 gather_fusion.3
  208.1 19.5 %all-to-all-done.4 = f32[256,1,8,128]{3,2,1,0:T(8,128)S(1)} async-done(((f32[256,1,8,128]{3,2,1,0:T(8,128)}), f32[256,1,8,128]{3,2,1,0:T(8,128)S(1)}, u32[]{:S(2)}, u32[]{:S(2)}) %all-to-all-start.4) | async-done | bytes 1048608 | tf_op jit(solution)/shard_map/all_to_all | solution.py:138
  228.0 0.7 copy_bitcast_fusion
  (100 shorter events, 10.1 us)
Async XLA Ops:
  0.6 41.1 %copy-start = (bf16[32,64,128]{2,1,0:T(8,128)(2,1)S(1)}, bf16[32,64,128]{2,1,0:T(8,128)(2,1)}, u32[]{:S(2)}) copy-start(bf16[32,64,128]{2,1,0:T(8,128)(2,1)} %param.13) | copy-start | bytes 1572868
  0.6 42.0 %copy-start.2 = (f32[32,1]{0,1:T(1,128)S(1)}, f32[32,1]{0,1:T(1,128)}, u32[]{:S(2)}) copy-start(f32[32,1]{0,1:T(1,128)} %param.16) | copy-start | bytes 388
  0.7 42.0 %copy-start.1 = (bf16[32,64,128]{2,1,0:T(8,128)(2,1)S(1)}, bf16[32,64,128]{2,1,0:T(8,128)(2,1)}, u32[]{:S(2)}) copy-start(bf16[32,64,128]{2,1,0:T(8,128)(2,1)} %param.14) | copy-start | bytes 1572868
  18.5 9.7 %all-to-all-start.3 = ((bf16[2,8,128]{2,0,1:T(2,128)(2,1)}), bf16[2,8,128]{2,0,1:T(2,128)(2,1)S(1)}, u32[]{:S(2)}, u32[]{:S(2)}) async-start(bf16[2,8,128]{2,0,1:T(2,128)(2,1)} %bitcast.155), calls=%async_computation.3 | async-start | bytes 8192 | tf_op jit(solution)/shard_map/all_to_all | solution.py:97
  29.1 27.6 %all-to-all-start.1 = ((bf16[16,16,1024]{2,1,0:T(8,128)(2,1)}), bf16[16,16,1024]{2,1,0:T(8,128)(2,1)S(1)}, u32[]{:S(2)}, u32[]{:S(2)}) async-start(bf16[16,16,1024]{2,1,0:T(8,128)(2,1)} %stack.5), calls=%async_computation.1 | async-start | bytes 1048576 | tf_op jit(solution)/shard_map/all_to_all | solution.py:103
  41.8 24.6 %copy-start.3 = (s32[32]{0:T(128)S(1)}, s32[32]{0:T(128)}, u32[]{:S(2)}) copy-start(s32[32]{0:T(128)} %param.17) | copy-start | bytes 388
  56.7 9.7 %all-to-all-start.2 = ((bf16[2,8,128]{2,0,1:T(2,128)(2,1)}), bf16[2,8,128]{2,0,1:T(2,128)(2,1)S(1)}, u32[]{:S(2)}, u32[]{:S(2)}) async-start(bf16[2,8,128]{2,0,1:T(2,128)(2,1)} %bitcast.5), calls=%async_computation.2 | async-start | bytes 8192 | tf_op jit(solution)/shard_map/all_to_all | solution.py:96
  67.0 73.0 %all-to-all-start.8 = ((s32[16,1,32]{2,1,0:T(1,128)}), s32[16,1,32]{2,1,0:T(1,128)S(1)}, u32[]{:S(2)}, u32[]{:S(2)}) async-start(s32[16,1,32]{2,1,0:T(1,128)} %broadcast_in_dim.50), calls=%async_computation.8 | async-start | bytes 16384 | tf_op jit(solution)/shard_map/all_to_all | solution.py:10
  140.0 14.2 %all-to-all-start.5 = ((f32[16,1,128]{2,1,0:T(1,128)}), f32[16,1,128]{2,1,0:T(1,128)S(1)}, u32[]{:S(2)}, u32[]{:S(2)}) async-start(f32[16,1,128]{2,1,0:T(1,128)} %reshape.186), calls=%async_computation.5 | async-start | bytes 16384 | tf_op jit(solution)/shard_map/all_to_all | solution.py:139
  154.2 10.9 %all-to-all-start.6 = ((f32[16,1,128]{2,1,0:T(1,128)}), f32[16,1,128]{2,1,0:T(1,128)S(1)}, u32[]{:S(2)}, u32[]{:S(2)}) async-start(f32[16,1,128]{2,1,0:T(1,128)} %reshape.188), calls=%async_computation.6 | async-start | bytes 16384 | tf_op jit(solution)/shard_map/all_to_all | solution.py:140
  196.8 30.9 %all-to-all-start.4 = ((f32[256,1,8,128]{3,2,1,0:T(8,128)}), f32[256,1,8,128]{3,2,1,0:T(8,128)S(1)}, u32[]{:S(2)}, u32[]{:S(2)}) async-start(f32[256,1,8,128]{3,2,1,0:T(8,128)} %bitcast.14), calls=%async_computation.4 | async-start | bytes 2097152 | tf_op jit(solution)/shard_map/all_to_all | solution.py:138
